TPU v7x, 32 devices: a whole 2x2x4 slice. The times are simulated.
32 devices in a mesh: row: 8 (over z, y), col: 4 (over x, core).
Axes of the slice: x: 2, y: 2, z: 4, core: 2. Of those that a mesh axis runs over, the one named last changes fastest.
Arguments:
- sequence: bfloat16 [128, 1024], P('row'), may hold values from -6 to 6
- pair_state: bfloat16 [128, 128, 128], P('row', 'col'), may hold values from -6 to 6
- residue_mask: int32 [128], replicated, may hold values 0 or 1
- chain_index: int32 [128], replicated, may hold values from 0 to 3, never falling along the last dimension, each value on 1 to 64 neighbouring positions
- attention_in: bfloat16 [1024, 4, 1024], P(None, None, 'col'), may hold values from -0.1875 to 0.1875
- attention_out: bfloat16 [1024, 1024], P('col'), may hold values from -0.1875 to 0.1875
- bias_weight: bfloat16 [128, 32], replicated, may hold values from -40 to 40
- chain_bias: float32 [32], replicated, may hold values from -2 to 2
- outer_in: bfloat16 [1024, 128], replicated, may hold values from -0.1875 to 0.1875
- outer_out: bfloat16 [128, 128], replicated, may hold values from -0.5 to 0.5
- triangle_in: bfloat16 [128, 5, 128], replicated, may hold values from -0.5 to 0.5
- triangle_out: bfloat16 [128, 128], replicated, may hold values from -0.5 to 0.5
- transition_up: bfloat16 [128, 512], replicated, may hold values from -0.5 to 0.5
- transition_down: bfloat16 [512, 128], replicated, may hold values from -0.25 to 0.25
Outputs:
- sequence_out: bfloat16 [128, 1024], P('row')
- pair_out: bfloat16 [128, 128, 128], P('row', 'col')
Inputs may be any that keep to these rules, and one draw needn't show every extreme that they name: chain_index never falls along the residues; each chain holds at most 64 residues.
All inputs are finite; a program needn't handle non-finite values.
Results may differ from a plain program's by a relative error of at most 0.0095.
The roundings to bfloat16 on the way count: a program that leaves them out, or rounds other values in their place, can miss the bound.
Values may be sent and summed in bfloat16 or wider, within the bound.
A program may use at most 64 MiB of HBM per device.

v0:
```python
import math
import jax
import jax.numpy as jnp
from jax import lax
from jax.sharding import PartitionSpec as P


def layer_norm(values):
    center = values - jnp.mean(values, axis=-1, keepdims=True)
    spread = jnp.mean(center * center, axis=-1, keepdims=True)
    return center * lax.rsqrt(spread + 1e-05)


def per_device(
    sequence,
    pair_state,
    residue_mask,
    chain_index,
    attention_in,
    attention_out,
    bias_weight,
    chain_bias,
    outer_in,
    outer_out,
    triangle_in,
    triangle_out,
    transition_up,
    transition_down,
):
    rows_here, cols_here, channels = pair_state.shape
    length_all = residue_mask.shape[0]
    row_index = lax.axis_index("row")
    col_index = lax.axis_index("col")
    row_start = row_index * rows_here
    col_start = col_index * cols_here
    pair_wide = pair_state.astype(jnp.float32)
    normed_pair = layer_norm(pair_wide).astype(jnp.bfloat16)
    bias_tile = jnp.einsum(
        "ijc,ch->hij", normed_pair, bias_weight, preferred_element_type=jnp.float32
    )
    pair_bias = lax.all_to_all(bias_tile, "col", split_axis=0, concat_axis=2, tiled=True)
    heads_here = pair_bias.shape[0]
    normed_seq = layer_norm(sequence.astype(jnp.float32)).astype(jnp.bfloat16)
    projected = jnp.einsum(
        "id,dpe->ipe", normed_seq, attention_in, preferred_element_type=jnp.float32
    )
    query = projected[:, 0].astype(jnp.bfloat16)
    key_rows = projected[:, 1].astype(jnp.bfloat16)
    value_rows = projected[:, 2].astype(jnp.bfloat16)
    gate = jax.nn.sigmoid(projected[:, 3])
    keys_all, values_all = (
        lax.all_gather(key_rows, "row", axis=0, tiled=True),
        lax.all_gather(value_rows, "row", axis=0, tiled=True),
    )
    head_width = query.shape[1] // heads_here
    query_heads = query.reshape(rows_here, heads_here, head_width)
    key_heads = keys_all.reshape(length_all, heads_here, head_width)
    value_heads = values_all.reshape(length_all, heads_here, head_width)
    scale = 1.0 / math.sqrt(head_width)
    scores = (
        jnp.einsum("ihd,jhd->hij", query_heads, key_heads, preferred_element_type=jnp.float32)
        * scale
    )
    chain_rows = lax.dynamic_slice_in_dim(chain_index, row_start, rows_here, 0)
    same_chain = (chain_rows[:, None] == chain_index[None, :]).astype(jnp.float32)
    head_offset = lax.dynamic_slice_in_dim(chain_bias, col_index * heads_here, heads_here, 0)
    scores = scores + pair_bias + head_offset[:, None, None] * same_chain[None]
    positions = jnp.arange(length_all, dtype=jnp.int32)
    query_ids = row_start + jnp.arange(rows_here, dtype=jnp.int32)
    allowed = (residue_mask[None, :] == 1) | (query_ids[:, None] == positions[None, :])
    allowed = allowed[None]
    highest = jnp.max(jnp.where(allowed, scores, -jnp.inf), axis=-1, keepdims=True)
    raised = jnp.where(allowed, jnp.exp(scores - highest), 0.0)
    weights = (raised / jnp.sum(raised, axis=-1, keepdims=True)).astype(jnp.bfloat16)
    gathered = jnp.einsum(
        "hij,jhd->ihd", weights, value_heads, preferred_element_type=jnp.float32
    ).reshape(rows_here, -1)
    mixed = (gate * gathered).astype(jnp.bfloat16)
    head_terms = jnp.dot(mixed, attention_out, preferred_element_type=jnp.float32)
    update = lax.psum(head_terms, "col")
    sequence_out = (sequence.astype(jnp.float32) + update).astype(jnp.bfloat16)
    normed_out = layer_norm(sequence_out.astype(jnp.float32)).astype(jnp.bfloat16)
    outer_rows = jnp.dot(normed_out, outer_in, preferred_element_type=jnp.float32).astype(
        jnp.bfloat16
    )
    half_width = outer_rows.shape[1] // 2
    right_all = lax.all_gather(outer_rows[:, half_width:], "row", axis=0, tiled=True)
    right_side = lax.dynamic_slice_in_dim(right_all, col_start, cols_here, 0).astype(jnp.float32)
    left_side = outer_rows[:, :half_width].astype(jnp.float32)
    outer_feat = jnp.concatenate(
        [
            left_side[:, None, :] * right_side[None, :, :],
            left_side[:, None, :] - right_side[None, :, :],
        ],
        axis=-1,
    ).astype(jnp.bfloat16)
    pair_mid = pair_wide + jnp.dot(
        outer_feat.reshape(-1, 2 * half_width), outer_out, preferred_element_type=jnp.float32
    ).reshape(rows_here, cols_here, channels)
    normed_mid = layer_norm(pair_mid).astype(jnp.bfloat16)
    tri = jnp.dot(
        normed_mid.reshape(-1, channels),
        triangle_in.reshape(channels, -1),
        preferred_element_type=jnp.float32,
    ).reshape(rows_here, cols_here, 5, channels)
    live = residue_mask.astype(jnp.float32)
    row_live = lax.dynamic_slice_in_dim(live, row_start, rows_here, 0)
    col_live = lax.dynamic_slice_in_dim(live, col_start, cols_here, 0)
    pair_live = (row_live[:, None] * col_live[None, :])[:, :, None]
    left_op = (jax.nn.sigmoid(tri[:, :, 0]) * tri[:, :, 1] * pair_live).astype(jnp.bfloat16)
    right_op = (jax.nn.sigmoid(tri[:, :, 2]) * tri[:, :, 3] * pair_live).astype(jnp.bfloat16)
    out_gate = jax.nn.sigmoid(tri[:, :, 4])
    column_all = lax.all_gather(right_op, "row", axis=0, tiled=True)
    crossed = lax.psum_scatter(
        jnp.einsum("jkc,ikc->jic", column_all, left_op, preferred_element_type=jnp.float32),
        "col",
        scatter_dimension=0,
        tiled=True,
    )
    product = jnp.transpose(crossed, (1, 0, 2))
    normed_product = layer_norm(product).astype(jnp.bfloat16)
    projected_product = jnp.dot(
        normed_product.reshape(-1, channels), triangle_out, preferred_element_type=jnp.float32
    ).reshape(rows_here, cols_here, channels)
    pair_late = pair_mid + out_gate * projected_product
    normed_late = layer_norm(pair_late).astype(jnp.bfloat16)
    hidden = jax.nn.relu(
        jnp.dot(
            normed_late.reshape(-1, channels), transition_up, preferred_element_type=jnp.float32
        )
    ).astype(jnp.bfloat16)
    lowered = jnp.dot(hidden, transition_down, preferred_element_type=jnp.float32).reshape(
        rows_here, cols_here, channels
    )
    pair_out = (pair_late + lowered).astype(jnp.bfloat16)
    return (sequence_out, pair_out)


def solution(mesh):
    return jax.shard_map(
        per_device,
        mesh=mesh,
        in_specs=(
            P("row", None),
            P("row", "col", None),
            P(),
            P(),
            P(None, None, "col"),
            P("col", None),
            P(),
            P(),
            P(),
            P(),
            P(),
            P(),
            P(),
            P(),
        ),
        out_specs=(P("row", None), P("row", "col", None)),
        check_vma=False,
    )
```

profile of v0, /device:TPU:0, one launch (start us, length us, event | category | flops | bytes accessed | tf_op | source)
XLA Modules:
  0.0 257.6 jit_solution(43655018280628967)
XLA Ops:
  7.2 1.2 convert_reduce_fusion
  8.4 1.2 fusion.14
  9.6 1.2 convolution_bitcast_fusion.1
  11.8 4.2 %all-to-all-start = ((f32[4,1,4096]{2,1,0:T(1,128)}), f32[4,1,4096]{2,1,0:T(1,128)S(1)}, u32[]{:S(2)}, u32[]{:S(2)}) async-start(f32[4,1,4096]{2,1,0:T(1,128)} %reshape.259), calls=%async_computation | async-start | bytes 131072 | tf_op jit(solution)/shard_map/all_to_all | solution.py:41
  21.9 1.9 fusion.92
  24.5 31.5 %all-gather.1 = bf16[128,1,256]{2,0,1:T(8,128)(2,1)S(1)} all-gather(bf16[16,1,256]{2,0,1:T(8,128)(2,1)S(1)} %get-tuple-element.7), channel_id=3, replica_groups=mesh['row'=8,'col'=4] {'row'}, dimensions={0}, use_global_device_ids=true | all-gather | bytes 73728 | tf_op jit(solution)/shard_map/all_gather | solution.py:52
  56.1 30.5 %all-gather = bf16[128,1,256]{2,0,1:T(8,128)(2,1)S(1)} all-gather(bf16[16,1,256]{2,0,1:T(8,128)(2,1)S(1)} %get-tuple-element.8), channel_id=2, replica_groups=mesh['row'=8,'col'=4] {'row'}, dimensions={0}, use_global_device_ids=true | all-gather | bytes 73728 | tf_op jit(solution)/shard_map/all_gather | solution.py:53
  90.4 1.1 convolution_bitcast_fusion.2
  91.6 1.5 fusion.74
  94.8 31.4 %all-reduce.2.cloned.1.call-done = f32[16,1024]{1,0:T(8,128)} async-done(((f32[16,1024]{1,0:T(8,128)}), f32[16,1024]{1,0:T(8,128)}) %all-reduce.2.cloned.1.call-update) | async-done | bytes 65552 | tf_op jit(solution)/shard_map/psum | solution.py:80
  127.7 30.7 %all_gather.14 = bf16[128,64]{1,0:T(8,128)(2,1)S(1)} all-gather(bf16[16,64]{1,0:T(8,128)(2,1)S(1)} %get-tuple-element.12), channel_id=1, replica_groups=mesh['row'=8,'col'=4] {'row'}, dimensions={0}, use_global_device_ids=true | all-gather | bytes 18432 | tf_op jit(solution)/shard_map/all_gather | solution.py:87
  158.4 1.1 fusion.94
  160.3 1.3 fusion.32
  162.5 1.2 copy.101
  163.7 39.1 %all-gather.4.cloned.1.call-done = bf16[128,32,128]{2,1,0:T(8,128)(2,1)} async-done(((bf16[16,32,128]{2,1,0:T(8,128)(2,1)}), bf16[128,32,128]{2,1,0:T(8,128)(2,1)}) %all-gather.4.cloned.1.call-update) | async-done | bytes 1048592 | tf_op jit(solution)/shard_map/all_gather | solution.py:113
  202.8 7.3 %copy.102 = bf16[128,32,128]{1,0,2:T(8,128)(2,1)} copy(bf16[128,32,128]{2,1,0:T(8,128)(2,1)} %all-gather.4.cloned.1.call-done) | data formatting | bytes 2097152 | tf_op jit(solution)/shard_map/all_gather | solution.py:113
  210.0 5.6 %convolution_bitcast_fusion = f32[128,16,128]{0,1,2:T(8,128)} fusion(bf16[16,32,128]{1,0,2:T(8,128)(2,1)} %copy.101, bf16[128,32,128]{1,0,2:T(8,128)(2,1)} %copy.102), kind=kOutput, calls=%fused_computation.4 | convolution fusion | flops 16777216 | bytes 2228224 | tf_op jit(solution)/shard_map/jkc,ikc->jic/dot_general | solution.py:115
  215.6 2.8 %copy.103 = f32[128,16,128]{2,1,0:T(8,128)} copy(f32[128,16,128]{0,1,2:T(8,128)} %convolution_bitcast_fusion) | data formatting | bytes 2097152 | tf_op jit(solution)/shard_map/jkc,ikc->jic/transpose | solution.py:115
  218.4 23.7 %reduce-scatter.2.cloned.1.call-done = f32[32,16,128]{2,1,0:T(8,128)} async-done(((f32[128,16,128]{2,1,0:T(8,128)}), f32[32,16,128]{2,1,0:T(8,128)}) %reduce-scatter.2.cloned.1.call-update) | async-done | bytes 262160 | tf_op jit(solution)/shard_map/reduce_scatter | solution.py:114
  243.4 1.2 multiply_reduce_fusion.1
  244.7 1.2 multiply_convert_fusion.1
  245.9 1.3 fusion.95
  248.1 1.3 fusion.4
  249.4 1.6 add_convert_fusion
  (84 shorter events, 18.5 us)
Async XLA Ops:
  7.2 14.7 %copy-start = (bf16[1024,4,256]{2,1,0:T(4,128)(2,1)S(1)}, bf16[1024,4,256]{2,1,0:T(4,128)(2,1)}, u32[]{:S(2)}) copy-start(bf16[1024,4,256]{2,1,0:T(4,128)(2,1)} %param.18) | copy-start | bytes 6291460
  9.6 77.8 %copy-start.10 = (f32[32]{0:T(128)S(1)}, f32[32]{0:T(128)}, u32[]{:S(2)}) copy-start(f32[32]{0:T(128)} %param.21) | copy-start | bytes 388
  11.8 75.7 %all-to-all-start = ((f32[4,1,4096]{2,1,0:T(1,128)}), f32[4,1,4096]{2,1,0:T(1,128)S(1)}, u32[]{:S(2)}, u32[]{:S(2)}) async-start(f32[4,1,4096]{2,1,0:T(1,128)} %reshape.259), calls=%async_computation | async-start | bytes 131072 | tf_op jit(solution)/shard_map/all_to_all | solution.py:41
  16.0 110.2 %all-reduce.2.cloned.1.call-start = ((), (), s32[]{:S(2)}) async-start(), calls=%async_computation.2 | async-start | bytes 131072 | tf_op jit(solution)/shard_map/psum | solution.py:80
  21.9 69.8 %copy-start.5 = (bf16[256,1024]{1,0:T(8,128)(2,1)S(1)}, bf16[256,1024]{1,0:T(8,128)(2,1)}, u32[]{:S(2)}) copy-start(bf16[256,1024]{1,0:T(8,128)(2,1)} %param.19) | copy-start | bytes 1572868
  23.7 70.3 %copy-start.6 = (bf16[128,5,128]{2,0,1:T(8,128)(2,1)S(1)}, bf16[128,5,128]{2,0,1:T(8,128)(2,1)}, u32[]{:S(2)}) copy-start(bf16[128,5,128]{2,0,1:T(8,128)(2,1)} %param.24) | copy-start | bytes 491524
  23.7 102.5 %copy-start.4 = (bf16[16,1024]{1,0:T(8,128)(2,1)S(1)}, bf16[16,1024]{1,0:T(8,128)(2,1)}, u32[]{:S(2)}) copy-start(bf16[16,1024]{1,0:T(8,128)(2,1)} %param.14) | copy-start | bytes 98308
  87.4 71.1 %copy-start.3 = (bf16[16,32,128]{2,1,0:T(8,128)(2,1)S(1)}, bf16[16,32,128]{2,1,0:T(8,128)(2,1)}, u32[]{:S(2)}) copy-start(bf16[16,32,128]{2,1,0:T(8,128)(2,1)} %param.15) | copy-start | bytes 393220
  89.2 38.2 %copy-start.8 = (bf16[1024,128]{1,0:T(8,128)(2,1)S(1)}, bf16[1024,128]{1,0:T(8,128)(2,1)}, u32[]{:S(2)}) copy-start(bf16[1024,128]{1,0:T(8,128)(2,1)} %param.22) | copy-start | bytes 786436
  93.2 109.6 %all-gather.4.cloned.1.call-start = ((), (), s32[]{:S(2)}) async-start(), calls=%async_computation.3 | async-start | bytes 1179648 | tf_op jit(solution)/shard_map/all_gather | solution.py:113
  127.2 32.6 %copy-start.7 = (bf16[16,1024]{1,0:T(8,128)(2,1)}, bf16[16,1024]{1,0:T(8,128)(2,1)S(1)}, u32[]{:S(2)}) copy-start(bf16[16,1024]{1,0:T(8,128)(2,1)S(1)} %get-tuple-element.3) | copy-start | bytes 98308
  159.5 0.7 copy-start.2
  162.4 79.7 %reduce-scatter.2.cloned.1.call-start = ((), (), s32[]{:S(2)}) async-start(), calls=%async_computation.4 | async-start | bytes 1310720 | tf_op jit(solution)/shard_map/reduce_scatter | solution.py:114
  245.9 2.2 copy-start.9
  247.2 0.7 copy-start.1
Sparse Core Ops, SparseCore 0:
  93.3 32.8 all-reduce.1
  162.5 40.1 all-gather.3
  218.6 23.5 reduce-scatter.1
where the time goes:
time: 259 us; the launch traced here: 258 us
  waiting for transfers between devices  94.3 us (36%)
  blocking collectives  92.7 us (36%)
  local copies, waits for them, and re-layouts  18.8 us (7%)
  matrix products  17.5 us (7%)
  other arithmetic  16 us (6%)
  between operations  14 us (5%)
  starting transfers between devices  4.32 us (2%)
    all_gather x1, waiting for transfers between devices, per_device(): column_all = lax.all_gather(right_op, 'row', axis=0, tiled=True)  39.1 us
    all_gather x1, blocking collectives, per_device(): lax.all_gather(key_rows, 'row', axis=0, tiled=True)  31.5 us
    psum x1, waiting for transfers between devices, per_device(): update = lax.psum(head_terms, 'col')  31.4 us
    all_gather x1, blocking collectives, per_device(): lax.all_gather(outer_rows[:, half_width:], 'row', axis=0, tiled=True)  30.7 us
    all_gather x1, blocking collectives, per_device(): lax.all_gather(value_rows, 'row', axis=0, tiled=True)  30.5 us
    reduce_scatter x1, waiting for transfers between devices, per_device(): lax.psum_scatter(jnp.einsum('jkc,ikc->jic', column_all, left_op, preferre...  23.7 us
    all_gather x1, local copies, waits for them, and re-layouts, per_device(): column_all = lax.all_gather(right_op, 'row', axis=0, tiled=True)  7.25 us
    dot_general x1, matrix products, per_device(): jnp.einsum('jkc,ikc->jic', column_all, left_op, preferred_element_type=jn...  5.6 us
  transfers between devices with their start and end apart: 4, of which 3 were waited for; matrix products, arithmetic and copies ran while one was open for 5% of the time, Pallas kernels for 0%

commit v1 on v0

--- a/solution.py
+++ b/solution.py
@@ -3,6 +3,21 @@
 import jax.numpy as jnp
 from jax import lax
 from jax.sharding import PartitionSpec as P
+
+
+def on_each_block(x, axis, dim, make, out_dim):
+    ways, here, step = (lax.axis_size(axis), lax.axis_index(axis), x.shape[dim])
+    results = []
+    for far in range(ways):
+        arriving = (
+            lax.ppermute(x, axis, [(d, (d + 1) % ways) for d in range(ways)])
+            if far + 1 < ways
+            else x
+        )
+        results.append(make(x, (here - far) % ways * step))
+        x = arriving
+    line = jnp.concatenate(results[::-1], axis=out_dim)
+    return jnp.roll(line, (here + 1) * results[0].shape[out_dim], axis=out_dim)
 
 
 def layer_norm(values):
@@ -110,9 +125,16 @@
     left_op = (jax.nn.sigmoid(tri[:, :, 0]) * tri[:, :, 1] * pair_live).astype(jnp.bfloat16)
     right_op = (jax.nn.sigmoid(tri[:, :, 2]) * tri[:, :, 3] * pair_live).astype(jnp.bfloat16)
     out_gate = jax.nn.sigmoid(tri[:, :, 4])
-    column_all = lax.all_gather(right_op, "row", axis=0, tiled=True)
     crossed = lax.psum_scatter(
-        jnp.einsum("jkc,ikc->jic", column_all, left_op, preferred_element_type=jnp.float32),
+        on_each_block(
+            right_op,
+            "row",
+            0,
+            lambda own_block, offset: jnp.einsum(
+                "jkc,ikc->jic", own_block, left_op, preferred_element_type=jnp.float32
+            ),
+            0,
+        ),
         "col",
         scatter_dimension=0,
         tiled=True,

time: 259 us -> 274 us (1.058)
  local copies, waits for them, and re-layouts: 18.8 us -> 32.3 us
  matrix products: 17.5 us -> 22.1 us
  waiting for transfers between devices: 94.3 us -> 90.5 us
    all_gather x1 -> x0, waiting for transfers between devices: 39.1 us -> none  [per_device(): column_all = lax.all_gather(right_op, 'row', axis=0, tiled=True)]
    ppermute x0 -> x7, waiting for transfers between devices: none -> 37.6 us  [on_each_block(): lax.ppermute(x, axis, [(d, (d + 1) % ways) for d in range(ways)])]
    concatenate x0 -> x1, local copies, waits for them, and re-layouts: none -> 13.1 us  [on_each_block(): return jnp.roll(line, (here + 1) * results[0].shape[out_dim], axis=out_dim)]
    all_gather x1 -> x0, local copies, waits for them, and re-layouts: 7.25 us -> none  [per_device(): column_all = lax.all_gather(right_op, 'row', axis=0, tiled=True)]
    ppermute x0 -> x7, local copies, waits for them, and re-layouts: none -> 6.69 us  [on_each_block(): lax.ppermute(x, axis, [(d, (d + 1) % ways) for d in range(ways)])]
    dot_general x1 -> x8, matrix products: 5.6 us -> 11.1 us  [per_device(): jnp.einsum('jkc,ikc->jic', own_block, left_op, preferred_element_type=jnp...]
    dynamic_slice x0 -> x2, local copies, waits for them, and re-layouts: none -> 3.54 us  [on_each_block(): return jnp.roll(line, (here + 1) * results[0].shape[out_dim], axis=out_dim)]
    reduce_scatter x1, waiting for transfers between devices: 23.7 us -> 20.8 us  [per_device(): lax.psum_scatter(on_each_block(right_op, 'row', 0, lambda own_block, offs...]
  transfers between devices with their start and end apart: 4 -> 10, of which waited for: 3 -> 9; matrix products, arithmetic and copies ran while one was open for 5% -> 10% of each run, Pallas kernels for 0% -> 0%
where the time goes in v1:
time: 274 us; the launch traced here: 273 us
  blocking collectives  92.7 us (34%)
  waiting for transfers between devices  90.5 us (33%)
  local copies, waits for them, and re-layouts  32.3 us (12%)
  matrix products  22.1 us (8%)
  other arithmetic  15.1 us (6%)
  between operations  14.4 us (5%)
  starting transfers between devices  5.77 us (2%)
    ppermute x7, waiting for transfers between devices, on_each_block(): lax.ppermute(x, axis, [(d, (d + 1) % ways) for d in range(ways)])  37.6 us
    psum x1, waiting for transfers between devices, per_device(): update = lax.psum(head_terms, 'col')  32.1 us
    all_gather x1, blocking collectives, per_device(): lax.all_gather(key_rows, 'row', axis=0, tiled=True)  31.5 us
    all_gather x1, blocking collectives, per_device(): lax.all_gather(outer_rows[:, half_width:], 'row', axis=0, tiled=True)  30.7 us
    all_gather x1, blocking collectives, per_device(): lax.all_gather(value_rows, 'row', axis=0, tiled=True)  30.5 us
    reduce_scatter x1, waiting for transfers between devices, per_device(): lax.psum_scatter(on_each_block(right_op, 'row', 0, lambda own_block, offs...  20.8 us
    concatenate x1, local copies, waits for them, and re-layouts, on_each_block(): return jnp.roll(line, (here + 1) * results[0].shape[out_dim], axis=out_dim)  13.1 us
    dot_general x8, matrix products, per_device(): jnp.einsum('jkc,ikc->jic', own_block, left_op, preferred_element_type=jnp...  11.1 us
  transfers between devices with their start and end apart: 10, of which 9 were waited for; matrix products, arithmetic and copies ran while one was open for 10% of the time, Pallas kernels for 0%

profile of v1, /device:TPU:0, one launch (start us, length us, event | category | flops | bytes accessed | tf_op | source)
XLA Modules:
  0.0 272.8 jit_solution(12061918019307983538)
XLA Ops:
  11.8 4.2 %all-to-all-start = ((f32[4,1,4096]{2,1,0:T(1,128)}), f32[4,1,4096]{2,1,0:T(1,128)S(1)}, u32[]{:S(2)}, u32[]{:S(2)}) async-start(f32[4,1,4096]{2,1,0:T(1,128)} %reshape.259), calls=%async_computation | async-start | bytes 131072 | tf_op jit(solution)/shard_map/all_to_all | solution.py:56
  21.9 1.9 fusion.92
  24.5 31.5 %all-gather.1 = bf16[128,1,256]{2,0,1:T(8,128)(2,1)S(1)} all-gather(bf16[16,1,256]{2,0,1:T(8,128)(2,1)S(1)} %get-tuple-element.7), channel_id=3, replica_groups=mesh['row'=8,'col'=4] {'row'}, dimensions={0}, use_global_device_ids=true | all-gather | bytes 73728 | tf_op jit(solution)/shard_map/all_gather | solution.py:67
  56.1 30.5 %all-gather = bf16[128,1,256]{2,0,1:T(8,128)(2,1)S(1)} all-gather(bf16[16,1,256]{2,0,1:T(8,128)(2,1)S(1)} %get-tuple-element.8), channel_id=2, replica_groups=mesh['row'=8,'col'=4] {'row'}, dimensions={0}, use_global_device_ids=true | all-gather | bytes 73728 | tf_op jit(solution)/shard_map/all_gather | solution.py:68
  91.6 1.5 fusion.74
  94.1 32.1 %all-reduce.2.cloned.1.call-done = f32[16,1024]{1,0:T(8,128)} async-done(((f32[16,1024]{1,0:T(8,128)}), f32[16,1024]{1,0:T(8,128)}) %all-reduce.2.cloned.1.call-update) | async-done | bytes 65552 | tf_op jit(solution)/shard_map/psum | solution.py:95
  128.6 30.7 %all_gather.11 = bf16[128,64]{1,0:T(8,128)(2,1)S(1)} all-gather(bf16[16,64]{1,0:T(8,128)(2,1)S(1)} %get-tuple-element.12), channel_id=1, replica_groups=mesh['row'=8,'col'=4] {'row'}, dimensions={0}, use_global_device_ids=true | all-gather | bytes 18432 | tf_op jit(solution)/shard_map/all_gather | solution.py:102
  163.0 1.5 collective-permute-start
  167.7 3.2 %collective-permute-done = bf16[16,32,128]{2,1,0:T(8,128)(2,1)} collective-permute-done((bf16[16,32,128]{2,1,0:T(8,128)(2,1)S(1)}, bf16[16,32,128]{2,1,0:T(8,128)(2,1)}, u32[]{:S(2)}, u32[]{:S(2)}) %collective-permute-start) | collective-permute-done | bytes 131104 | tf_op jit(solution)/shard_map/ppermute | solution.py:13
  172.2 1.4 convolution_bitcast_fusion.1
  173.6 5.1 %collective-permute-done.1 = bf16[16,32,128]{2,1,0:T(8,128)(2,1)S(1)} collective-permute-done((bf16[16,32,128]{2,1,0:T(8,128)(2,1)}, bf16[16,32,128]{2,1,0:T(8,128)(2,1)S(1)}, u32[]{:S(2)}, u32[]{:S(2)}) %collective-permute-start.1) | collective-permute-done | bytes 131104 | tf_op jit(solution)/shard_map/ppermute | solution.py:13
  179.1 1.4 convolution_bitcast_fusion.2
  180.5 5.9 %collective-permute-done.2 = bf16[16,32,128]{2,1,0:T(8,128)(2,1)} collective-permute-done((bf16[16,32,128]{2,1,0:T(8,128)(2,1)S(1)}, bf16[16,32,128]{2,1,0:T(8,128)(2,1)}, u32[]{:S(2)}, u32[]{:S(2)}) %collective-permute-start.2) | collective-permute-done | bytes 131104 | tf_op jit(solution)/shard_map/ppermute | solution.py:13
  187.8 1.4 convolution_bitcast_fusion.3
  189.2 5.2 %collective-permute-done.3 = bf16[16,32,128]{2,1,0:T(8,128)(2,1)S(1)} collective-permute-done((bf16[16,32,128]{2,1,0:T(8,128)(2,1)}, bf16[16,32,128]{2,1,0:T(8,128)(2,1)S(1)}, u32[]{:S(2)}, u32[]{:S(2)}) %collective-permute-start.3) | collective-permute-done | bytes 131104 | tf_op jit(solution)/shard_map/ppermute | solution.py:13
  194.9 1.5 convolution_bitcast_fusion.4
  196.3 7.1 %collective-permute-done.4 = bf16[16,32,128]{2,1,0:T(8,128)(2,1)} collective-permute-done((bf16[16,32,128]{2,1,0:T(8,128)(2,1)S(1)}, bf16[16,32,128]{2,1,0:T(8,128)(2,1)}, u32[]{:S(2)}, u32[]{:S(2)}) %collective-permute-start.4) | collective-permute-done | bytes 131104 | tf_op jit(solution)/shard_map/ppermute | solution.py:13
  204.8 1.4 convolution_bitcast_fusion.5
  206.2 5.1 %collective-permute-done.5 = bf16[16,32,128]{2,1,0:T(8,128)(2,1)S(1)} collective-permute-done((bf16[16,32,128]{2,1,0:T(8,128)(2,1)}, bf16[16,32,128]{2,1,0:T(8,128)(2,1)S(1)}, u32[]{:S(2)}, u32[]{:S(2)}) %collective-permute-start.5) | collective-permute-done | bytes 131104 | tf_op jit(solution)/shard_map/ppermute | solution.py:13
  213.1 6.0 %collective-permute-done.6 = bf16[16,32,128]{2,1,0:T(8,128)(2,1)} collective-permute-done((bf16[16,32,128]{2,1,0:T(8,128)(2,1)S(1)}, bf16[16,32,128]{2,1,0:T(8,128)(2,1)}, u32[]{:S(2)}, u32[]{:S(2)}) %collective-permute-start.6) | collective-permute-done | bytes 131104 | tf_op jit(solution)/shard_map/ppermute | solution.py:13
  221.8 13.1 %concatenate.13 = f32[256,16,128]{0,1,2:T(8,128)} concatenate(f32[16,16,128]{0,1,2:T(8,128)} %convolution_bitcast_fusion.7, f32[16,16,128]{0,1,2:T(8,128)} %convolution_bitcast_fusion.6, f32[16,16,128]{0,1,2:T(8,128)} %convolution_bitcast_fusion.5, f32[16,16,128]{0,1,2:T(8,128)} %convolution_bitcast_fusion.4, f32[16,16,128]{0,1,2:T(8,128)} %convolution_bitcast_fusion.3, ...), dimensions={0} | concatenate | bytes 4194304 | tf_op jit(solution)/shard_map/jit(_roll_dynamic)/concatenate | solution.py:20
  234.9 1.9 constant_dynamic-slice_fusion
  236.8 1.6 copy.173
  238.5 20.8 %reduce-scatter.2.cloned.1.call-done = f32[32,16,128]{2,1,0:T(8,128)} async-done(((f32[128,16,128]{2,1,0:T(8,128)}), f32[32,16,128]{2,1,0:T(8,128)}) %reduce-scatter.2.cloned.1.call-update) | async-done | bytes 262160 | tf_op jit(solution)/shard_map/reduce_scatter | solution.py:128
  (111 shorter events, 42.5 us)
Async XLA Ops:
  7.2 14.7 %copy-start = (bf16[1024,4,256]{2,1,0:T(4,128)(2,1)S(1)}, bf16[1024,4,256]{2,1,0:T(4,128)(2,1)}, u32[]{:S(2)}) copy-start(bf16[1024,4,256]{2,1,0:T(4,128)(2,1)} %param.18) | copy-start | bytes 6291460
  9.6 77.8 %copy-start.10 = (f32[32]{0:T(128)S(1)}, f32[32]{0:T(128)}, u32[]{:S(2)}) copy-start(f32[32]{0:T(128)} %param.21) | copy-start | bytes 388
  11.8 75.7 %all-to-all-start = ((f32[4,1,4096]{2,1,0:T(1,128)}), f32[4,1,4096]{2,1,0:T(1,128)S(1)}, u32[]{:S(2)}, u32[]{:S(2)}) async-start(f32[4,1,4096]{2,1,0:T(1,128)} %reshape.259), calls=%async_computation | async-start | bytes 131072 | tf_op jit(solution)/shard_map/all_to_all | solution.py:56
  16.0 110.2 %all-reduce.2.cloned.1.call-start = ((), (), s32[]{:S(2)}) async-start(), calls=%async_computation.2 | async-start | bytes 131072 | tf_op jit(solution)/shard_map/psum | solution.py:95
  21.9 69.8 %copy-start.4 = (bf16[256,1024]{1,0:T(8,128)(2,1)S(1)}, bf16[256,1024]{1,0:T(8,128)(2,1)}, u32[]{:S(2)}) copy-start(bf16[256,1024]{1,0:T(8,128)(2,1)} %param.19) | copy-start | bytes 1572868
  23.7 70.2 %copy-start.5 = (bf16[128,5,128]{2,0,1:T(8,128)(2,1)S(1)}, bf16[128,5,128]{2,0,1:T(8,128)(2,1)}, u32[]{:S(2)}) copy-start(bf16[128,5,128]{2,0,1:T(8,128)(2,1)} %param.24) | copy-start | bytes 491524
  23.7 102.5 %copy-start.3 = (bf16[16,1024]{1,0:T(8,128)(2,1)S(1)}, bf16[16,1024]{1,0:T(8,128)(2,1)}, u32[]{:S(2)}) copy-start(bf16[16,1024]{1,0:T(8,128)(2,1)} %param.14) | copy-start | bytes 98308
  88.0 71.4 %copy-start.2 = (bf16[16,32,128]{2,1,0:T(8,128)(2,1)S(1)}, bf16[16,32,128]{2,1,0:T(8,128)(2,1)}, u32[]{:S(2)}) copy-start(bf16[16,32,128]{2,1,0:T(8,128)(2,1)} %param.15) | copy-start | bytes 393220
  93.2 166.1 %reduce-scatter.2.cloned.1.call-start = ((), (), s32[]{:S(2)}) async-start(), calls=%async_computation.3 | async-start | bytes 1310720 | tf_op jit(solution)/shard_map/reduce_scatter | solution.py:128
  127.2 32.1 %copy-start.6 = (bf16[16,1024]{1,0:T(8,128)(2,1)}, bf16[16,1024]{1,0:T(8,128)(2,1)S(1)}, u32[]{:S(2)}) copy-start(bf16[16,1024]{1,0:T(8,128)(2,1)S(1)} %get-tuple-element.3) | copy-start | bytes 98308
  161.2 1.1 copy-start.1
  163.0 7.8 %collective-permute-start = (bf16[16,32,128]{2,1,0:T(8,128)(2,1)S(1)}, bf16[16,32,128]{2,1,0:T(8,128)(2,1)}, u32[]{:S(2)}, u32[]{:S(2)}) collective-permute-start(bf16[16,32,128]{2,1,0:T(8,128)(2,1)S(1)} %get-tuple-element.4), channel_id=1, source_target_pairs={{0,4},{4,8},{8,12},{12,16},{16,20},{20,24},{24,28},{28,0},{1,5},{5... | collective-permute-start | bytes 393224 | tf_op jit(solution)/shard_map/ppermute | solution.py:13
  170.8 7.9 %collective-permute-start.1 = (bf16[16,32,128]{2,1,0:T(8,128)(2,1)}, bf16[16,32,128]{2,1,0:T(8,128)(2,1)S(1)}, u32[]{:S(2)}, u32[]{:S(2)}) collective-permute-start(bf16[16,32,128]{2,1,0:T(8,128)(2,1)} %collective-permute-done), channel_id=1, source_target_pairs={{0,4},{4,8},{8,12},{12,16},{16,20},{20,24},{24,28},{28,0},{1,5},{5... | collective-permute-start | bytes 393224 | tf_op jit(solution)/shard_map/ppermute | solution.py:13
  178.7 7.8 %collective-permute-start.2 = (bf16[16,32,128]{2,1,0:T(8,128)(2,1)S(1)}, bf16[16,32,128]{2,1,0:T(8,128)(2,1)}, u32[]{:S(2)}, u32[]{:S(2)}) collective-permute-start(bf16[16,32,128]{2,1,0:T(8,128)(2,1)S(1)} %collective-permute-done.1), channel_id=1, source_target_pairs={{0,4},{4,8},{8,12},{12,16},{16,20},{20,24},{24,28},{28,0},{1,5},{5... | collective-permute-start | bytes 393224 | tf_op jit(solution)/shard_map/ppermute | solution.py:13
  186.5 8.0 %collective-permute-start.3 = (bf16[16,32,128]{2,1,0:T(8,128)(2,1)}, bf16[16,32,128]{2,1,0:T(8,128)(2,1)S(1)}, u32[]{:S(2)}, u32[]{:S(2)}) collective-permute-start(bf16[16,32,128]{2,1,0:T(8,128)(2,1)} %collective-permute-done.2), channel_id=1, source_target_pairs={{0,4},{4,8},{8,12},{12,16},{16,20},{20,24},{24,28},{28,0},{1,5},{5... | collective-permute-start | bytes 393224 | tf_op jit(solution)/shard_map/ppermute | solution.py:13
  194.4 9.0 %collective-permute-start.4 = (bf16[16,32,128]{2,1,0:T(8,128)(2,1)S(1)}, bf16[16,32,128]{2,1,0:T(8,128)(2,1)}, u32[]{:S(2)}, u32[]{:S(2)}) collective-permute-start(bf16[16,32,128]{2,1,0:T(8,128)(2,1)S(1)} %collective-permute-done.3), channel_id=1, source_target_pairs={{0,4},{4,8},{8,12},{12,16},{16,20},{20,24},{24,28},{28,0},{1,5},{5... | collective-permute-start | bytes 393224 | tf_op jit(solution)/shard_map/ppermute | solution.py:13
  203.4 7.9 %collective-permute-start.5 = (bf16[16,32,128]{2,1,0:T(8,128)(2,1)}, bf16[16,32,128]{2,1,0:T(8,128)(2,1)S(1)}, u32[]{:S(2)}, u32[]{:S(2)}) collective-permute-start(bf16[16,32,128]{2,1,0:T(8,128)(2,1)} %collective-permute-done.4), channel_id=1, source_target_pairs={{0,4},{4,8},{8,12},{12,16},{16,20},{20,24},{24,28},{28,0},{1,5},{5... | collective-permute-start | bytes 393224 | tf_op jit(solution)/shard_map/ppermute | solution.py:13
  211.3 7.8 %collective-permute-start.6 = (bf16[16,32,128]{2,1,0:T(8,128)(2,1)S(1)}, bf16[16,32,128]{2,1,0:T(8,128)(2,1)}, u32[]{:S(2)}, u32[]{:S(2)}) collective-permute-start(bf16[16,32,128]{2,1,0:T(8,128)(2,1)S(1)} %collective-permute-done.5), channel_id=1, source_target_pairs={{0,4},{4,8},{8,12},{12,16},{16,20},{20,24},{24,28},{28,0},{1,5},{5... | collective-permute-start | bytes 393224 | tf_op jit(solution)/shard_map/ppermute | solution.py:13
  236.8 26.2 %copy-start.9 = (bf16[128,128]{1,0:T(8,128)(2,1)S(1)}, bf16[128,128]{1,0:T(8,128)(2,1)}, u32[]{:S(2)}) copy-start(bf16[128,128]{1,0:T(8,128)(2,1)} %param.25) | copy-start | bytes 98308
  238.4 26.3 %copy-start.7 = (bf16[512,128]{1,0:T(8,128)(2,1)S(1)}, bf16[512,128]{1,0:T(8,128)(2,1)}, u32[]{:S(2)}) copy-start(bf16[512,128]{1,0:T(8,128)(2,1)} %param.27) | copy-start | bytes 393220
  238.4 26.4 %copy-start.8 = (bf16[128,512]{1,0:T(8,128)(2,1)S(1)}, bf16[128,512]{1,0:T(8,128)(2,1)}, u32[]{:S(2)}) copy-start(bf16[128,512]{1,0:T(8,128)(2,1)} %param.26) | copy-start | bytes 393220
Sparse Core Ops, SparseCore 0:
  93.3 32.8 all-reduce.1
  238.6 20.6 reduce-scatter.1
